TPU v7x, 256 devices: a whole 4x4x8 slice. The times are simulated.
256 devices in a mesh: gx: 16 (over x, z_hi), gy: 4 (over y), gz: 4 (over z_lo, core).
Axes of the slice: x: 4, y: 4, z: 8 (z_hi: 4, z_lo: 2; z = z_hi * 2 + z_lo), core: 2. Of those that a mesh axis runs over, the one named last changes fastest.
Arguments:
- flow_field: bfloat16 [512, 256, 2048], P('gx', 'gy', 'gz'), may hold values from -96 to 96
- left_x: bfloat16 [512, 128], P('gx'), may hold values from -0.0234375 to 0.0234375
- last_x: bfloat16 [512, 128], P('gx'), may hold values from -0.25 to 0.25
- last_y: bfloat16 [256, 128], P('gy'), may hold values from -0.005859375 to 0.005859375
- right_y: bfloat16 [256, 256], P('gy'), may hold values from -0.375 to 0.375
- right_m: bfloat16 [2048, 256], P('gz'), may hold values from -0.125 to 0.125
- last_m: bfloat16 [2048, 256], P('gz'), may hold values from -0.125 to 0.125
Outputs:
- core_first: float32 [512, 128], P('gx')
- core_middle: float32 [128, 256, 128], P(('gx', 'gz'), 'gy')
- core_last: float32 [128, 2048], P(None, 'gz')
All inputs are finite; a program needn't handle non-finite values.
Results may differ from a plain program's by a relative error of at most 0.0053.
Values sent between devices are 32-bit elements; how exact they have to be, the bound alone decides.
A program may use at most 64 MiB of HBM per device.

v0:
```python
import jax
import jax.numpy as jnp
from jax import lax
from jax.sharding import PartitionSpec as P


def normal_solve(system, right_side):
    gram_matrix = jnp.dot(system, system.T, precision=lax.Precision.HIGHEST)
    factor = jnp.linalg.cholesky(gram_matrix)
    return jax.scipy.linalg.cho_solve((factor, True), right_side)


def per_device(flow_field, left_x, last_x, last_y, right_y, right_m, last_m):
    highest = lax.Precision.HIGHEST
    x_cells, y_cells, m_cells = flow_field.shape
    rank_cols = left_x.shape[1]
    sketch_cols = right_m.shape[1]
    flat_field = flow_field.reshape(x_cells * y_cells, m_cells)
    first_terms = jnp.dot(flat_field, right_m, preferred_element_type=jnp.float32).reshape(
        x_cells, y_cells, sketch_cols
    )
    first_part = jnp.sum(first_terms * right_y.astype(jnp.float32)[None], axis=1)
    first_rows = lax.psum(first_part, ("gy", "gz"))
    left_wide = left_x.astype(jnp.float32)
    first_gram = lax.psum(jnp.dot(left_wide.T, first_rows, precision=highest), "gx")
    core_first = normal_solve(first_gram, jnp.dot(first_gram, first_rows.T, precision=highest)).T
    khatri = (last_x.astype(jnp.float32)[:, None, :] * last_y.astype(jnp.float32)[None]).astype(
        jnp.bfloat16
    )
    khatri = khatri.reshape(x_cells * y_cells, rank_cols)
    last_part = jnp.dot(khatri.T, flat_field, preferred_element_type=jnp.float32)
    core_last = lax.psum(last_part, ("gx", "gy"))
    last_gram = lax.psum(jnp.dot(core_last, last_m.astype(jnp.float32), precision=highest), "gz")
    pinv_last = normal_solve(last_gram, last_gram).T
    flat_terms = jnp.dot(flat_field, last_m, preferred_element_type=jnp.float32)
    last_terms = flat_terms.reshape(x_cells, y_cells * sketch_cols)
    row_share = rank_cols // lax.axis_size(("gx", "gz"))
    middle_sums = lax.psum_scatter(
        jnp.dot(left_wide.T, last_terms, precision=highest).reshape(
            row_share * lax.axis_size(("gx", "gz")), y_cells, sketch_cols
        ),
        ("gx", "gz"),
        scatter_dimension=0,
        tiled=True,
    )
    core_middle = jnp.dot(
        middle_sums.reshape(row_share * y_cells, sketch_cols), pinv_last, precision=highest
    )
    core_middle = core_middle.reshape(row_share, y_cells, rank_cols)
    return (core_first, core_middle, core_last)


def solution(mesh):
    return jax.shard_map(
        per_device,
        mesh=mesh,
        in_specs=(
            P("gx", "gy", "gz"),
            P("gx", None),
            P("gx", None),
            P("gy", None),
            P("gy", None),
            P("gz", None),
            P("gz", None),
        ),
        out_specs=(P("gx", None), P(("gx", "gz"), "gy", None), P(None, "gz")),
        check_vma=False,
    )
```

profile of v0, /device:TPU:1, one launch (start us, length us, event | category | flops | bytes accessed | tf_op | source)
XLA Modules:
  0.0 930.0 jit_solution(4668367135638992668)
XLA Ops:
  8.0 0.0 copy-start
  8.0 0.0 copy-start.4
  8.0 0.0 copy-start.5
  8.0 0.0 all-reduce.6.cloned.1.call-start
  8.1 0.9 convert_element_type.16
  9.0 0.7 convert_element_type.15
  9.7 0.0 copy-done
  9.7 1.2 convolution_bitcast_fusion
  10.8 0.0 all-reduce.6.cloned.1.call-update
  10.9 0.0 all-reduce.4.cloned.1.call-start
  10.9 0.0 copy-start.3
  11.0 0.0 copy-start.2
  11.0 0.7 multiply_reduce_fusion
  11.7 54.8 %psum.28 = f32[32,256]{1,0:T(8,128)S(1)} all-reduce(f32[32,256]{1,0:T(8,128)S(1)} %multiply_reduce_fusion), channel_id=1, replica_groups=mesh['gx'=16,'gy'=4,'gz'=4] {'gy','gz'}, use_global_device_ids=true, to_apply=%region_1.0 | all-reduce | flops 8192 | bytes 65536 | tf_op jit(solution)/shard_map/psum | solution.py:23
  66.5 0.9 convolution_bitcast_fusion.2
  67.5 0.0 all-reduce.4.cloned.1.call-update
  67.5 0.0 all-reduce.8.cloned.1.call-start
  67.5 2.0 fusion.16
  69.5 2.8 reshape.46
  72.3 589.0 %all-reduce.6.cloned.1.call-done = f32[128,512]{1,0:T(8,128)} async-done(((f32[128,512]{1,0:T(8,128)}), f32[128,512]{1,0:T(8,128)}) %all-reduce.6.cloned.1.call-update) | async-done | bytes 262160 | tf_op jit(solution)/shard_map/psum | solution.py:32
  661.3 1.9 fusion.18
  663.2 0.0 all-reduce.8.cloned.1.call-update
  663.3 0.0 reduce-scatter.2.cloned.1.call-start
  663.3 10.1 %fusion.17 = f32[16384,128]{1,0:T(8,128)} fusion(f32[32,16384]{1,0:T(8,128)} %reshape.46, bf16[32,128]{1,0:T(8,128)(2,1)S(1)} %copy-done.3), kind=kOutput, calls=%fused_computation.32 | convolution fusion | flops 805306368 | bytes 10493952 | tf_op jit(solution)/shard_map/dot_general | solution.py:39
  673.4 9.2 copy.11
  682.6 0.0 reduce-scatter.2.cloned.1.call-update
  682.6 161.7 %all-reduce.4.cloned.1.call-done = f32[128,256]{0,1:T(8,128)} async-done(((f32[128,256]{0,1:T(8,128)}), f32[128,256]{0,1:T(8,128)}) %all-reduce.4.cloned.1.call-update) | async-done | bytes 131088 | tf_op jit(solution)/shard_map/psum | solution.py:25
  844.3 1.4 fusion.14
  845.6 0.1 copy.10
  845.8 11.7 %cholesky.44 = f32[128,128]{1,0:T(8,128)S(1)} custom-call(f32[128,128]{1,0:T(8,128)S(1)} %fusion.13), custom_call_target="Cholesky" | custom-call | tf_op jit(solution)/shard_map/jit(cholesky)/cholesky | solution.py:9
  857.5 0.6 compare_reduce_fusion.1
  858.1 0.7 fusion.3
  858.8 9.8 %custom-call.16 = f32[1,128,128]{1,2,0:T(8,128)S(1)} custom-call(f32[1,128,128]{2,1,0:T(8,128)S(1)} %fusion.3), custom_call_target="InvertDiagBlocksLowerTriangular" | custom-call | tf_op jit(solution)/shard_map/jit(_cho_solve)/triangular_solve | solution.py:10
  868.6 1.3 fusion.15
  869.9 0.3 fusion.11
  870.2 0.9 fusion.9
  871.1 23.5 %all-reduce.8.cloned.1.call-done = f32[128,256]{1,0:T(8,128)} async-done(((f32[128,256]{1,0:T(8,128)}), f32[128,256]{1,0:T(8,128)}) %all-reduce.8.cloned.1.call-update) | async-done | bytes 131088 | tf_op jit(solution)/shard_map/psum | solution.py:33
  894.5 1.3 fusion.19
  895.8 0.1 copy.12
  895.9 11.7 %cholesky.55 = f32[128,128]{1,0:T(8,128)S(1)} custom-call(f32[128,128]{1,0:T(8,128)S(1)} %fusion.8), custom_call_target="Cholesky" | custom-call | tf_op jit(solution)/shard_map/jit(cholesky)/cholesky | solution.py:9
  907.7 0.6 compare_reduce_fusion
  908.3 0.7 fusion.4
  909.0 9.8 %custom-call.17 = f32[1,128,128]{1,2,0:T(8,128)S(1)} custom-call(f32[1,128,128]{2,1,0:T(8,128)S(1)} %fusion.4), custom_call_target="InvertDiagBlocksLowerTriangular" | custom-call | tf_op jit(solution)/shard_map/jit(_cho_solve)/triangular_solve | solution.py:10
  918.8 1.2 fusion.6
  920.0 0.3 convolution_bitcast_fusion.1
  920.3 0.0 reduce-scatter.2.cloned.1.call-done
  920.3 1.8 fusion.20
  922.1 0.7 copy.16
  (11 shorter events, 0.1 us)
Async XLA Ops:
  8.0 1.7 copy-start
  8.0 2.9 copy-start.4
  8.0 2.9 copy-start.5
  8.0 653.3 %all-reduce.6.cloned.1.call-start = ((), (), s32[]{:S(2)}) async-start(), calls=%async_computation.3 | async-start | bytes 524288 | tf_op jit(solution)/shard_map/psum | solution.py:32
  10.9 833.4 %all-reduce.4.cloned.1.call-start = ((), (), s32[]{:S(2)}) async-start(), calls=%async_computation.1 | async-start | bytes 262144 | tf_op jit(solution)/shard_map/psum | solution.py:25
  10.9 55.6 %copy-start.3 = (bf16[32,128]{1,0:T(8,128)(2,1)S(1)}, bf16[32,128]{1,0:T(8,128)(2,1)}, u32[]{:S(2)}) copy-start(bf16[32,128]{1,0:T(8,128)(2,1)} %param.9) | copy-start | bytes 24580
  11.0 56.6 %copy-start.2 = (bf16[512,256]{1,0:T(8,128)(2,1)S(1)}, bf16[512,256]{1,0:T(8,128)(2,1)}, u32[]{:S(2)}) copy-start(bf16[512,256]{1,0:T(8,128)(2,1)} %param.14) | copy-start | bytes 786436
  67.5 827.1 %all-reduce.8.cloned.1.call-start = ((), (), s32[]{:S(2)}) async-start(), calls=%async_computation.4 | async-start | bytes 262144 | tf_op jit(solution)/shard_map/psum | solution.py:33
  663.3 257.1 %reduce-scatter.2.cloned.1.call-start = ((), (), s32[]{:S(2)}) async-start(), calls=%async_computation.2 | async-start | bytes 8519680 | tf_op jit(solution)/shard_map/reduce_scatter | solution.py:38
  682.6 239.5 %copy-start.1 = (f32[128,512]{1,0:T(8,128)S(1)}, f32[128,512]{1,0:T(8,128)}, u32[]{:S(2)}) copy-start(f32[128,512]{1,0:T(8,128)} %all-reduce.6.cloned.1.call-done) | copy-start | bytes 786436
Sparse Core Ops, SparseCore 0:
  12.1 649.2 all-reduce.5
  664.1 180.0 all-reduce.3
  847.7 46.8 all-reduce.7
Sparse Core Ops, SparseCore 1:
  682.7 170.6 reduce-scatter.1
where the time goes:
time: 930 us
  waiting for transfers between devices  774 us (83%)
  blocking collectives  54.8 us (6%)
  other arithmetic  47.3 us (5%)
  matrix products  25.1 us (3%)
  between operations  15.4 us (2%)
  local copies, waits for them, and re-layouts  12.9 us (1%)
    psum x1, waiting for transfers between devices, per_device(): core_last = lax.psum(last_part, ('gx', 'gy'))  589 us
    psum x1, waiting for transfers between devices, per_device(): lax.psum(jnp.dot(left_wide.T, first_rows, precision=highest), 'gx')  162 us
    psum x1, blocking collectives, per_device(): first_rows = lax.psum(first_part, ('gy', 'gz'))  54.8 us
    another operation x6, other arithmetic, normal_solve(): factor = jnp.linalg.cholesky(gram_matrix)  24.8 us
    psum x1, waiting for transfers between devices, per_device(): lax.psum(jnp.dot(core_last, last_m.astype(jnp.float32), precision=highest...  23.5 us
    another operation x4, other arithmetic, normal_solve(): return jax.scipy.linalg.cho_solve((factor, True), right_side)  20.9 us
  transfers between devices with their start and end apart: 4, of which 3 were waited for; matrix products, arithmetic and copies ran while one was open for 9% of the time, Pallas kernels for 0%

commit v1 on v0

v1 whole, which is shorter than its diff:
```python
import functools

import jax
import jax.numpy as jnp
from jax import lax
from jax.experimental import pallas as pl
from jax.experimental.pallas import tpu as pltpu
from jax.sharding import PartitionSpec as P

HIGHEST = lax.Precision.HIGHEST
NT = (((1,), (1,)), ((), ()))


def dot_nt(left, right, precision=HIGHEST):
    return lax.dot_general(
        left, right, NT, precision=precision, preferred_element_type=jnp.float32
    )


def split_dot(left, right):
    high = right.astype(jnp.bfloat16)
    low = (right - high.astype(jnp.float32)).astype(jnp.bfloat16)
    return jnp.dot(left, high, preferred_element_type=jnp.float32) + jnp.dot(
        left, low, preferred_element_type=jnp.float32
    )


def row_order(size):
    p = lax.broadcasted_iota(jnp.int32, (size, size), 0)
    rest, x, zl, core, zh = p & 1, (p >> 1) & 3, (p >> 3) & 1, (p >> 4) & 1, p >> 5
    a = (x << 5) + (zh << 3) + (zl << 2) + (core << 1) + rest
    lane = lax.broadcasted_iota(jnp.int32, (size, size), 1)
    return jnp.where(lane == a, 1.0, 0.0).astype(jnp.bfloat16)


def sweep_steps(mat, first, last):
    size = mat.shape[0]
    lane = lax.broadcasted_iota(jnp.int32, (size, size), 1)
    sub = lax.broadcasted_iota(jnp.int32, (size, size), 0)

    def step(k, carry):
        now = mat[...]
        row = mat[pl.ds(k, 1), :]
        here = lane == k
        col = jnp.sum(jnp.where(here, now, 0.0), axis=1, keepdims=True)
        pivot = jnp.sum(jnp.where(lane[:1] == k, row, 0.0), axis=1, keepdims=True)
        inv = 1.0 / pivot
        row_new = jnp.where(lane[:1] == k, 1.0, row) * inv
        kept = jnp.where(here, 0.0, now)
        mat[...] = jnp.where(sub == k, row_new, kept - col * row_new)
        return carry

    lax.fori_loop(first, last, step, 0)


def exchange_kernel(
    t_ref, z_ref, cl_ref, yf_ref, lx_ref, first_out, middle_out, last_out,
    z0, zs, z1, z1s, z2, z2s, zfull, qall, mat,
    c1, c1s, c2, cfull,
    y0, y0s, y1, y1s, y2,
    lxall, t0, ts, t1, t1s, t2, yp, t3, y3, y4, mm, obuf,
    send_sems, recv_sems,
):
    gx, gy, gz = lax.axis_index("gx"), lax.axis_index("gy"), lax.axis_index("gz")
    x, zh = gx // 4, gx % 4
    y = gy
    zl, core = gz // 2, gz % 2
    pos_xy = x * 4 + y
    pos_z = zh * 2 + zl
    pos_g = zl * 4 + x
    count = [0]

    def at(x_=None, y_=None, zh_=None, zl_=None, core_=None):
        x_ = x if x_ is None else x_
        y_ = y if y_ is None else y_
        zh_ = zh if zh_ is None else zh_
        zl_ = zl if zl_ is None else zl_
        core_ = core if core_ is None else core_
        return (x_ * 4 + zh_, y_, zl_ * 2 + core_)

    def send(src, dst, device):
        n = count[0]
        count[0] += 1
        copy = pltpu.make_async_remote_copy(
            src_ref=src, dst_ref=dst, send_sem=send_sems.at[n], recv_sem=recv_sems.at[n],
            device_id=device, device_id_type=pl.DeviceIdType.MESH,
        )
        copy.start()
        started.append(copy)
        return copy

    started = []

    def peer_xy(d):
        q = (pos_xy + d) % 16
        return q, at(x_=q // 4, y_=q % 4)

    def peer_z(d):
        q = (pos_z + d) % 8
        return q, at(zh_=q // 2, zl_=q % 2)

    def peer_g(d):
        q = (pos_g + d) % 8
        return q, at(zl_=q // 4, x_=q % 4)

    other_core = at(core_=1 - core)
    other_zl = at(zl_=1 - zl)

    barrier = pltpu.get_barrier_semaphore()
    greeted = [peer_xy(d)[1] for d in range(1, 16)] + [peer_z(d)[1] for d in range(1, 8)]
    greeted += [other_core]
    greeted += [at(zl_=1 - zl, x_=(x + d) % 4) for d in range(1, 4)]
    for device in greeted:
        pl.semaphore_signal(
            barrier, inc=1, device_id=device, device_id_type=pl.DeviceIdType.MESH
        )
    pl.semaphore_wait(barrier, len(greeted))

    z_core = send(z_ref.at[1 - core], z0, other_core)
    y_core = send(yf_ref, y0, other_core)
    t_core = {}
    for half in (1, 0):
        for d in (1, 2, 3, 0):
            j0 = pl.multiple_of(((zl + half) % 2) * 32 + ((x + d) % 4) * 8, 8)
            t_core[half, d] = send(
                t_ref.at[:, pl.ds(j0, 8), pl.ds(128, 128)], t0.at[half * 4 + d], other_core
            )
    lx_x = [send(lx_ref, lxall.at[x], at(x_=(x + d) % 4)) for d in range(1, 4)]
    lxall[x] = lx_ref[...]

    z_core.wait_recv()
    zs[...] = z_ref[core] + z0[...]
    z_xy = []
    for d in range(1, 16):
        q, device = peer_xy(d)
        z_xy.append(send(zs.at[pl.ds(pl.multiple_of(q * 8, 8), 8)], z1.at[d], device))
    c_xy = []
    for d in range(1, 16):
        q, device = peer_xy(d)
        c_xy.append(send(cl_ref.at[pl.ds(pl.multiple_of(q * 8, 8), 8)], c1.at[d], device))
    own_xy = pl.ds(pl.multiple_of(pos_xy * 8, 8), 8)

    def t_sum(half, d):
        t_core[half, d].wait_recv()
        j0 = pl.multiple_of(((zl + half) % 2) * 32 + ((x + d) % 4) * 8, 8)
        mine = t_ref[:, pl.ds(j0, 8), 0:128]
        ts[half * 4 + d] = (mine + t0[half * 4 + d]).reshape(256, 128)

    t_zl = {}
    for d in (1, 2):
        t_sum(1, d)
        t_zl[d] = send(ts.at[4 + d], t1.at[d], other_zl)
    y_core.wait_recv()
    y0s[...] = yf_ref[...] + y0[...]
    for d in (3, 0):
        t_sum(1, d)
    for d in (1, 2, 3, 0):
        t_sum(0, d)

    for copy in z_xy:
        copy.wait_recv()
    total = zs[own_xy]
    for d in range(1, 16):
        total = total + z1[d]
    z1s[...] = total
    z_z = []
    for d in range(1, 8):
        z_z.append(send(z1s, z2.at[d], peer_z(d)[1]))
    y_zl = send(y0s, y1, other_zl)
    for d in (3, 0):
        t_zl[d] = send(ts.at[4 + d], t1.at[d], other_zl)

    for copy in c_xy:
        copy.wait_recv()
    total = cl_ref[own_xy]
    for d in range(1, 16):
        total = total + c1[d]
    c1s[...] = total
    t_x = {}

    def t_forward(d):
        t_zl[d].wait_recv()
        t1s[d] = ts[d] + t1[d]
        if d:
            t_x[d] = send(
                t1s.at[d],
                t2.at[pl.ds(pl.multiple_of(x * 256, 256), 256)],
                at(x_=(x + d) % 4),
            )
        else:
            t2[pl.ds(pl.multiple_of(x * 256, 256), 256), :] = t1s[d]

    for d in (1, 2):
        t_forward(d)

    for copy in z_z:
        copy.wait_recv()
    total = z1s[...]
    for d in range(1, 8):
        total = total + z2[d]
    z2s[...] = total
    z_all = []
    for d in range(1, 16):
        z_all.append(send(z2s, zfull.at[own_xy], peer_xy(d)[1]))
    zfull[own_xy] = total
    c_z = [send(c1s, c2.at[d], at(zh_=(zh + d) % 4)) for d in range(1, 4)]
    y_zl.wait_recv()
    y1s[...] = y0s[...] + y1[...]
    y_y = [send(y1s, y2.at[d], at(y_=(y + d) % 4)) for d in range(1, 4)]
    for d in (3, 0):
        t_forward(d)
    for copy in lx_x:
        copy.wait_recv()
    left = dot_nt(
        row_order(128), lxall[...].reshape(128, 128).astype(jnp.bfloat16), None
    ).astype(jnp.bfloat16)

    for copy in z_all:
        copy.wait_recv()
    mat[...] = dot_nt(zfull[...], zfull[...])

    sweep_steps(mat, 0, 32)

    for copy in c_z:
        copy.wait_recv()
    total = c1s[...]
    for d in range(1, 4):
        total = total + c2[d]
    cfull[own_xy] = total
    c_all = []
    for d in range(1, 16):
        c_all.append(send(cfull.at[own_xy], cfull.at[own_xy], peer_xy(d)[1]))
    for copy in t_x.values():
        copy.wait_recv()
    for j in range(8):
        rows = pl.ds(j, 128, stride=8)
        yp[rows, :] = split_dot(left, t2[rows, :])
    t_zh = []
    for d in range(1, 4):
        q = (zh + d) % 4
        t_zh.append(
            send(yp.at[pl.ds(pl.multiple_of(q * 256, 256), 256)], t3.at[d], at(zh_=q))
        )

    sweep_steps(mat, 32, 128)

    inverse = mat[...]
    qall[core] = jnp.dot(
        inverse, zfull[...], precision=HIGHEST, preferred_element_type=jnp.float32
    )
    q_core = send(qall.at[core], qall.at[core], other_core)

    for copy in t_zh:
        copy.wait_recv()
    total = yp[pl.ds(pl.multiple_of(zh * 256, 256), 256), :]
    for d in range(1, 4):
        total = total + t3[d]
    y3[...] = total
    m_core = send(
        y3.at[pl.ds(pl.multiple_of((1 - core) * 128, 128), 128)], y4.at[core], other_core
    )
    y4[core] = y3[pl.ds(pl.multiple_of(core * 128, 128), 128), :]
    for copy in y_y:
        copy.wait_recv()
    total = y1s[...]
    for d in range(1, 4):
        total = total + y2[d]
    q_core.wait_recv()
    m_core.wait_recv()
    mixed = dot_nt(y4[0], qall[1, :, 0:128]) + dot_nt(y4[1], qall[1, :, 128:256])
    mm[...] = mixed.reshape(16, 8, 128)
    m_all = []
    own_j = pl.ds(pl.multiple_of(pos_g * 8, 8), 8)
    for d in range(1, 8):
        q, device = peer_g(d)
        m_all.append(send(mm.at[pl.ds(q * 2, 2)], obuf.at[:, own_j, :], device))
    obuf[:, own_j, :] = mm[pl.ds(pos_g * 2, 2)]
    first_out[...] = dot_nt(total, qall[0])
    for copy in c_all:
        copy.wait_recv()
    last_out[...] = cfull[...]
    for copy in m_all:
        copy.wait_recv()
    middle_out[...] = obuf[...]
    for copy in started:
        copy.wait_send()


COPIES = 1 + 1 + 8 + 3 + 15 + 15 + 4 + 7 + 1 + 3 + 15 + 3 + 3 + 15 + 3 + 1 + 1 + 7


def exchange(t_part, z_part, cl_part, yf_part, left_wide):
    f32 = jnp.float32
    shapes = [
        (128, 256), (128, 256), (16, 8, 256), (8, 256), (8, 8, 256), (8, 256), (128, 256),
        (2, 128, 256), (128, 128),
        (16, 8, 512), (8, 512), (4, 8, 512), (128, 512),
        (32, 256), (32, 256), (32, 256), (32, 256), (4, 32, 256),
        (4, 32, 128), (8, 32, 8, 128), (8, 256, 128), (4, 256, 128), (4, 256, 128),
        (1024, 128), (1024, 128), (4, 256, 128), (256, 128), (2, 128, 128),
        (16, 8, 128), (2, 64, 128),
    ]
    vmem = pl.BlockSpec(memory_space=pltpu.VMEM)
    return pl.pallas_call(
        exchange_kernel,
        out_shape=(
            jax.ShapeDtypeStruct((32, 128), f32),
            jax.ShapeDtypeStruct((2, 64, 128), f32),
            jax.ShapeDtypeStruct((128, 512), f32),
        ),
        in_specs=[vmem] * 5,
        out_specs=(vmem,) * 3,
        scratch_shapes=[pltpu.VMEM(shape, f32) for shape in shapes]
        + [pltpu.SemaphoreType.DMA((COPIES,)), pltpu.SemaphoreType.DMA((COPIES,))],
        compiler_params=pltpu.CompilerParams(
            collective_id=0, has_side_effects=True, vmem_limit_bytes=32 * 1024 * 1024
        ),
        name="exchange",
    )(t_part, z_part, cl_part, yf_part, left_wide)


def per_device(flow_field, left_x, last_x, last_y, right_y, right_m, last_m):
    x_cells, y_cells, m_cells = flow_field.shape
    rank_cols = left_x.shape[1]
    sketch_cols = right_m.shape[1]
    core = lax.axis_index("gz") % 2
    flat_field = flow_field.reshape(x_cells * y_cells, m_cells)
    first_terms = jnp.dot(flat_field, right_m, preferred_element_type=jnp.float32).reshape(
        x_cells, y_cells, sketch_cols
    )
    first_part = jnp.sum(first_terms * right_y.astype(jnp.float32)[None], axis=1)
    left_wide = left_x.astype(jnp.float32)
    z_first = jnp.dot(left_wide.T, first_part, precision=HIGHEST)
    khatri = (last_x.astype(jnp.float32)[:, None, :] * last_y.astype(jnp.float32)[None]).astype(
        jnp.bfloat16
    )
    khatri = khatri.reshape(x_cells * y_cells, rank_cols)
    last_part = jnp.dot(khatri.T, flat_field, preferred_element_type=jnp.float32)
    z_last = jnp.dot(last_part, last_m.astype(jnp.float32), precision=HIGHEST)
    z_part = jnp.stack([z_first, z_last])
    half = sketch_cols // 2
    own_m = jnp.where(core == 0, last_m[:, :half], last_m[:, half:])
    other_m = jnp.where(core == 0, last_m[:, half:], last_m[:, :half])
    own_first = jnp.concatenate([own_m, other_m], axis=1)
    t_part = jnp.dot(flat_field, own_first, preferred_element_type=jnp.float32).reshape(
        x_cells, y_cells, sketch_cols
    )
    return exchange(t_part, z_part, last_part, first_part, left_wide)


def solution(mesh):
    return jax.shard_map(
        per_device,
        mesh=mesh,
        in_specs=(
            P("gx", "gy", "gz"),
            P("gx", None),
            P("gx", None),
            P("gy", None),
            P("gy", None),
            P("gz", None),
            P("gz", None),
        ),
        out_specs=(P("gx", None), P(("gx", "gz"), "gy", None), P(None, "gz")),
        check_vma=False,
    )
```

time: 930 us -> 66.2 us (0.07)
  waiting for transfers between devices: 774 us -> 0 us
  blocking collectives: 54.8 us -> 0 us
  Pallas kernels: 0 us -> 53.8 us
  other arithmetic: 47.3 us -> 1.18 us
  matrix products: 25.1 us -> 3.85 us
  between operations: 15.4 us -> 0.79 us
    psum x3 -> x0, waiting for transfers between devices: 774 us -> none  [the longest x1 589 us: per_device(): core_last = lax.psum(last_part, ('gx', 'gy'))]
    psum x1 -> x0, blocking collectives: 54.8 us -> none  [per_device(): first_rows = lax.psum(first_part, ('gy', 'gz'))]
    pallas_call x0 -> x1, Pallas kernels: none -> 53.8 us  [exchange(): pl.pallas_call(exchange_kernel, out_shape=(jax.ShapeDtypeStruct((32, 128)...]
    another operation x10 -> x1, other arithmetic: 45.7 us -> 0.02 us  [per_device(): z_part = jnp.stack([z_first, z_last])]
    dot_general x8 -> x3, matrix products: 20.6 us -> 2.67 us  [the longest x1 2.13 us: per_device(): jnp.dot(flat_field, own_first, preferred_element_type=jnp.float32)]
    reshape x2 -> x0, local copies, waits for them, and re-layouts: 12 us -> none  [the longest x1 9.18 us: per_device(): jnp.dot(left_wide.T, last_terms, precision=highest)]
  transfers between devices with their start and end apart: 4 -> 0, of which waited for: 3 -> 0; matrix products, arithmetic and copies ran while one was open for 9% -> 0% of each run, Pallas kernels for 0% -> 0%
where the time goes in v1:
time: 66.2 us; the launch traced here: 66 us
  Pallas kernels  53.8 us (81%)
  local copies, waits for them, and re-layouts  6.42 us (10%)
  matrix products  3.85 us (6%)
  other arithmetic  1.18 us (2%)
  between operations  0.79 us (1%)
    pallas_call x1, Pallas kernels, exchange(): pl.pallas_call(exchange_kernel, out_shape=(jax.ShapeDtypeStruct((32, 128)...  53.8 us
    unnamed x19, local copies, waits for them, and re-layouts  3.5 us
    dot_general x1, local copies, waits for them, and re-layouts, per_device(): jnp.dot(flat_field, own_first, preferred_element_type=jnp.float32)  2.92 us
    dot_general x1, matrix products, per_device(): jnp.dot(flat_field, own_first, preferred_element_type=jnp.float32)  2.13 us

profile of v1, /device:TPU:1, one launch (start us, length us, event | category | flops | bytes accessed | tf_op | source)
XLA Modules:
  0.0 66.0 jit_solution(18201785411658219279)
XLA Ops:
  0.6 0.0 copy-start
  0.7 1.1 %broadcast_select_fusion.1 = (bf16[512,128]{1,0:T(8,128)(2,1)S(1)}, bf16[512,128]{1,0:T(8,128)(2,1)S(1)}) fusion(pred[]{:T(512)S(6)} %eq.6, bf16[512,256]{1,0:T(8,128)(2,1)} %param.13), kind=kLoop, calls=%fused_computation.14 | loop fusion | flops 131072 | bytes 524289 | tf_op jit(solution)/shard_map/jit(_where)/select_n | solution.py:342
  1.8 0.6 copy-done
  2.4 2.1 %convolution_bitcast_fusion = f32[2048,256]{0,1:T(8,128)} fusion(bf16[2048,512]{1,0:T(8,128)(2,1)S(1)} %bitcast.22, bf16[512,128]{1,0:T(8,128)(2,1)S(1)} %get-tuple-element.4, bf16[512,128]{1,0:T(8,128)(2,1)S(1)} %get-tuple-element.3), kind=kOutput, calls=%fused_computation | convolution fusion | flops 537395200 | bytes 4456448 | tf_op jit(solution)/shard_map/dot_general | solution.py:345
  4.5 0.0 copy-start.5
  4.5 0.0 copy-start.6
  4.5 2.9 %copy.10 = f32[2048,256]{1,0:T(8,128)} copy(f32[2048,256]{0,1:T(8,128)} %convolution_bitcast_fusion) | data formatting | bytes 4194304 | tf_op jit(solution)/shard_map/dot_general | solution.py:345
  7.4 0.0 copy-start.2
  7.4 0.0 copy-start.3
  7.4 0.0 copy-start.7
  7.4 0.0 copy-done.5
  7.4 0.0 copy-done.6
  7.5 0.5 convolution_bitcast_fusion.1.cl_ref
  7.9 0.4 copy-done.2
  8.4 0.3 convolution_bitcast_fusion.2
  8.6 0.0 copy-done.3
  8.7 0.0 copy-start.4
  8.7 0.0 copy-done.7
  8.7 0.0 copy-start.1
  8.7 0.7 %multiply_reduce_fusion.yf_ref = f32[32,256]{1,0:T(8,128)S(1)} fusion(bf16[32,64,512]{2,1,0:T(8,128)(2,1)S(1)} %copy-done, f32[64,256]{1,0:T(8,128)S(1)} %convert_element_type.16, bf16[512,256]{1,0:T(8,128)(2,1)S(1)} %copy-done.7), kind=kOutput, calls=%fused_computation.1 | convolution fusion | flops 537911296 | bytes 2457600 | tf_op jit(solution)/shard_map/dot_general | solution.py:328
  9.4 0.0 copy-done.4
  9.4 0.3 convolution_bitcast_fusion.3
  9.7 0.5 copy-done.1
  10.3 53.8 %exchange.1 = (f32[32,128]{1,0:T(8,128)S(1)}, f32[2,64,128]{2,1,0:T(8,128)S(1)}, f32[128,512]{1,0:T(8,128)S(1)}) custom-call(f32[32,64,256]{2,1,0:T(8,128)S(1)} %bitcast.23, f32[2,128,256]{2,1,0:T(8,128)S(1)} %pad_maximum_fusion.z_ref, f32[128,512]{1,0:T(8,128)S(1)} %convolution_bitcast_fusion.1.cl_ref, f32[32,256]{1,0:T(8,128)S(1)} %multiply_reduce_fusion.yf_ref, ...), custom_call_target="tpu_custom_call" | custom-call | tf_op jit(solution)/shard_map/exchange/pallas_call | solution.py:304
  64.1 0.6 copy.16
  64.7 0.6 copy.17
  65.3 0.7 %copy.18 = f32[128,512]{1,0:T(8,128)} copy(f32[128,512]{1,0:T(8,128)S(1)} %get-tuple-element.10) | data formatting | bytes 524288
  (5 shorter events, 0.0 us)
Async XLA Ops:
  0.6 1.7 %copy-start = (bf16[32,64,512]{2,1,0:T(8,128)(2,1)S(1)}, bf16[32,64,512]{2,1,0:T(8,128)(2,1)}, u32[]{:S(2)}) copy-start(bf16[32,64,512]{2,1,0:T(8,128)(2,1)} %param.7) | copy-start | bytes 6291460
  4.5 2.9 %copy-start.5 = (bf16[64,128]{1,0:T(8,128)(2,1)S(1)}, bf16[64,128]{1,0:T(8,128)(2,1)}, u32[]{:S(2)}) copy-start(bf16[64,128]{1,0:T(8,128)(2,1)} %param.10) | copy-start | bytes 49156
  4.5 3.0 %copy-start.6 = (bf16[32,128]{1,0:T(8,128)(2,1)S(1)}, bf16[32,128]{1,0:T(8,128)(2,1)}, u32[]{:S(2)}) copy-start(bf16[32,128]{1,0:T(8,128)(2,1)} %param.9) | copy-start | bytes 24580
  7.4 0.9 %copy-start.2 = (bf16[512,256]{1,0:T(8,128)(2,1)S(1)}, bf16[512,256]{1,0:T(8,128)(2,1)}, u32[]{:S(2)}) copy-start(bf16[512,256]{1,0:T(8,128)(2,1)} %param.13) | copy-start | bytes 786436
  7.4 1.2 %copy-start.3 = (bf16[64,256]{1,0:T(8,128)(2,1)S(1)}, bf16[64,256]{1,0:T(8,128)(2,1)}, u32[]{:S(2)}) copy-start(bf16[64,256]{1,0:T(8,128)(2,1)} %param.11) | copy-start | bytes 98308
  7.4 1.3 %copy-start.7 = (bf16[512,256]{1,0:T(8,128)(2,1)S(1)}, bf16[512,256]{1,0:T(8,128)(2,1)}, u32[]{:S(2)}) copy-start(bf16[512,256]{1,0:T(8,128)(2,1)} %param.12) | copy-start | bytes 786436
  8.7 0.8 %copy-start.4 = (bf16[32,128]{1,0:T(8,128)(2,1)S(1)}, bf16[32,128]{1,0:T(8,128)(2,1)}, u32[]{:S(2)}) copy-start(bf16[32,128]{1,0:T(8,128)(2,1)} %param.8) | copy-start | bytes 24580
  8.7 1.6 %copy-start.1 = (f32[2048,256]{1,0:T(8,128)S(1)}, f32[2048,256]{1,0:T(8,128)}, u32[]{:S(2)}) copy-start(f32[2048,256]{1,0:T(8,128)} %copy.10) | copy-start | bytes 6291460

commit v2 on v1

--- a/solution.py
+++ b/solution.py
@@ -1,5 +1,3 @@
-import functools
-
 import jax
 import jax.numpy as jnp
 from jax import lax
@@ -9,6 +7,8 @@
 
 HIGHEST = lax.Precision.HIGHEST
 NT = (((1,), (1,)), ((), ()))
+TN = (((0,), (0,)), ((), ()))
+CELLS = 4
 
 
 def dot_nt(left, right, precision=HIGHEST):
@@ -23,6 +23,18 @@
     return jnp.dot(left, high, preferred_element_type=jnp.float32) + jnp.dot(
         left, low, preferred_element_type=jnp.float32
     )
+
+
+def three_parts(value):
+    high = value.astype(jnp.bfloat16)
+    rest = value - high.astype(jnp.float32)
+    middle = rest.astype(jnp.bfloat16)
+    low = (rest - middle.astype(jnp.float32)).astype(jnp.bfloat16)
+    return high, middle, low
+
+
+def dot_tn(left, right):
+    return lax.dot_general(left, right, TN, preferred_element_type=jnp.float32)
 
 
 def row_order(size):
@@ -54,12 +66,15 @@
 
 
 def exchange_kernel(
-    t_ref, z_ref, cl_ref, yf_ref, lx_ref, first_out, middle_out, last_out,
+    field_hbm, left_x_hbm, last_x_hbm, last_y_hbm, right_y_hbm, right_m_hbm, last_m_hbm,
+    first_out, middle_out, last_out,
+    field, left_x, last_x, last_y, right_y, right_m, last_m, kh,
+    t_ref, z_ref, cl_ref, yf_ref, lx_ref,
     z0, zs, z1, z1s, z2, z2s, zfull, qall, mat,
     c1, c1s, c2, cfull,
     y0, y0s, y1, y1s, y2,
     lxall, t0, ts, t1, t1s, t2, yp, t3, y3, y4, mm, obuf,
-    send_sems, recv_sems,
+    send_sems, recv_sems, load_sems,
 ):
     gx, gy, gz = lax.axis_index("gx"), lax.axis_index("gy"), lax.axis_index("gz")
     x, zh = gx // 4, gx % 4
@@ -114,16 +129,62 @@
         pl.semaphore_signal(
             barrier, inc=1, device_id=device, device_id_type=pl.DeviceIdType.MESH
         )
+    loads = [
+        pltpu.make_async_copy(src, dst, load_sems.at[n])
+        for n, (src, dst) in enumerate(
+            (
+                (last_x_hbm, last_x), (last_y_hbm, last_y), (right_y_hbm, right_y),
+                (left_x_hbm, left_x), (field_hbm, field), (right_m_hbm, right_m),
+                (last_m_hbm, last_m),
+            )
+        )
+    ]
+    for copy in loads:
+        copy.start()
+    for copy in loads[:4]:
+        copy.wait()
+    lx_ref[...] = left_x[...].astype(jnp.float32)
+    y_cells = last_y.shape[0]
+    last_x_wide = last_x[...].astype(jnp.float32)
+    last_y_wide = last_y[...].astype(jnp.float32)
+    for i in range(last_x.shape[0]):
+        kh[i * y_cells : (i + 1) * y_cells] = (
+            last_x_wide[i : i + 1] * last_y_wide
+        ).astype(jnp.bfloat16)
+    for copy in loads[4:]:
+        copy.wait()
+    cl_ref[...] = dot_tn(kh[...], field[...])
+    weights = right_y[...].astype(jnp.float32)[None]
+    for i in range(0, left_x.shape[0], CELLS):
+        terms = jnp.dot(
+            field[i * y_cells : (i + CELLS) * y_cells], right_m[...],
+            preferred_element_type=jnp.float32,
+        )
+        yf_ref[i : i + CELLS] = jnp.sum(
+            terms.reshape(CELLS, y_cells, terms.shape[1]) * weights, axis=1
+        )
+    z_ref[0] = sum(dot_tn(left_x[...], part) for part in three_parts(yf_ref[...]))
+    z_ref[1] = sum(
+        jnp.dot(part, last_m[...], preferred_element_type=jnp.float32)
+        for part in three_parts(cl_ref[...])
+    )
     pl.semaphore_wait(barrier, len(greeted))
 
     z_core = send(z_ref.at[1 - core], z0, other_core)
     y_core = send(yf_ref, y0, other_core)
+    for i in range(0, left_x.shape[0], CELLS):
+        terms = jnp.dot(
+            field[i * y_cells : (i + CELLS) * y_cells], last_m[...],
+            preferred_element_type=jnp.float32,
+        ).reshape(CELLS, y_cells, 256)
+        for c in range(2):
+            t_ref[c, i : i + CELLS] = terms[:, :, c * 128 : (c + 1) * 128]
     t_core = {}
     for half in (1, 0):
         for d in (1, 2, 3, 0):
             j0 = pl.multiple_of(((zl + half) % 2) * 32 + ((x + d) % 4) * 8, 8)
             t_core[half, d] = send(
-                t_ref.at[:, pl.ds(j0, 8), pl.ds(128, 128)], t0.at[half * 4 + d], other_core
+                t_ref.at[1 - core, :, pl.ds(j0, 8)], t0.at[half * 4 + d], other_core
             )
     lx_x = [send(lx_ref, lxall.at[x], at(x_=(x + d) % 4)) for d in range(1, 4)]
     lxall[x] = lx_ref[...]
@@ -143,7 +204,7 @@
     def t_sum(half, d):
         t_core[half, d].wait_recv()
         j0 = pl.multiple_of(((zl + half) % 2) * 32 + ((x + d) % 4) * 8, 8)
-        mine = t_ref[:, pl.ds(j0, 8), 0:128]
+        mine = t_ref[core, :, pl.ds(j0, 8), :]
         ts[half * 4 + d] = (mine + t0[half * 4 + d]).reshape(256, 128)
 
     t_zl = {}
@@ -289,9 +350,12 @@
 COPIES = 1 + 1 + 8 + 3 + 15 + 15 + 4 + 7 + 1 + 3 + 15 + 3 + 3 + 15 + 3 + 1 + 1 + 7
 
 
-def exchange(t_part, z_part, cl_part, yf_part, left_wide):
+def per_device(flow_field, left_x, last_x, last_y, right_y, right_m, last_m):
     f32 = jnp.float32
+    flat_field = flow_field.reshape(-1, flow_field.shape[2])
+    inputs = (flat_field, left_x, last_x, last_y, right_y, right_m, last_m)
     shapes = [
+        (2, 32, 64, 128), (2, 128, 256), (128, 512), (32, 256), (32, 128),
         (128, 256), (128, 256), (16, 8, 256), (8, 256), (8, 8, 256), (8, 256), (128, 256),
         (2, 128, 256), (128, 128),
         (16, 8, 512), (8, 512), (4, 8, 512), (128, 512),
@@ -308,44 +372,17 @@
             jax.ShapeDtypeStruct((2, 64, 128), f32),
             jax.ShapeDtypeStruct((128, 512), f32),
         ),
-        in_specs=[vmem] * 5,
+        in_specs=[pl.BlockSpec(memory_space=pl.ANY)] * 7,
         out_specs=(vmem,) * 3,
-        scratch_shapes=[pltpu.VMEM(shape, f32) for shape in shapes]
-        + [pltpu.SemaphoreType.DMA((COPIES,)), pltpu.SemaphoreType.DMA((COPIES,))],
+        scratch_shapes=[pltpu.VMEM(array.shape, jnp.bfloat16) for array in inputs]
+        + [pltpu.VMEM((2048, 128), jnp.bfloat16)]
+        + [pltpu.VMEM(shape, f32) for shape in shapes]
+        + [pltpu.SemaphoreType.DMA((count,)) for count in (COPIES, COPIES, 7)],
         compiler_params=pltpu.CompilerParams(
             collective_id=0, has_side_effects=True, vmem_limit_bytes=32 * 1024 * 1024
         ),
         name="exchange",
-    )(t_part, z_part, cl_part, yf_part, left_wide)
-
-
-def per_device(flow_field, left_x, last_x, last_y, right_y, right_m, last_m):
-    x_cells, y_cells, m_cells = flow_field.shape
-    rank_cols = left_x.shape[1]
-    sketch_cols = right_m.shape[1]
-    core = lax.axis_index("gz") % 2
-    flat_field = flow_field.reshape(x_cells * y_cells, m_cells)
-    first_terms = jnp.dot(flat_field, right_m, preferred_element_type=jnp.float32).reshape(
-        x_cells, y_cells, sketch_cols
-    )
-    first_part = jnp.sum(first_terms * right_y.astype(jnp.float32)[None], axis=1)
-    left_wide = left_x.astype(jnp.float32)
-    z_first = jnp.dot(left_wide.T, first_part, precision=HIGHEST)
-    khatri = (last_x.astype(jnp.float32)[:, None, :] * last_y.astype(jnp.float32)[None]).astype(
-        jnp.bfloat16
-    )
-    khatri = khatri.reshape(x_cells * y_cells, rank_cols)
-    last_part = jnp.dot(khatri.T, flat_field, preferred_element_type=jnp.float32)
-    z_last = jnp.dot(last_part, last_m.astype(jnp.float32), precision=HIGHEST)
-    z_part = jnp.stack([z_first, z_last])
-    half = sketch_cols // 2
-    own_m = jnp.where(core == 0, last_m[:, :half], last_m[:, half:])
-    other_m = jnp.where(core == 0, last_m[:, half:], last_m[:, :half])
-    own_first = jnp.concatenate([own_m, other_m], axis=1)
-    t_part = jnp.dot(flat_field, own_first, preferred_element_type=jnp.float32).reshape(
-        x_cells, y_cells, sketch_cols
-    )
-    return exchange(t_part, z_part, last_part, first_part, left_wide)
+    )(*inputs)
 
 
 def solution(mesh):

time: 66.2 us -> 62.6 us (0.946)
  matrix products: 3.85 us -> 0 us
  local copies, waits for them, and re-layouts: 6.42 us -> 8.29 us
  other arithmetic: 1.18 us -> 0 us
    unnamed x19 -> x17, local copies, waits for them, and re-layouts: 3.5 us -> 8.29 us
    dot_general x5 -> x0, matrix products: 3.85 us -> none  [the longest x1 2.13 us: per_device(): jnp.dot(flat_field, own_first, preferred_element_type=jnp.float32)]
    dot_general x1 -> x0, local copies, waits for them, and re-layouts: 2.92 us -> none  [per_device(): jnp.dot(flat_field, own_first, preferred_element_type=jnp.float32)]
    select_n x1 -> x0, other arithmetic: 1.14 us -> none  [per_device(): own_m = jnp.where(core == 0, last_m[:, :half], last_m[:, half:])]
where the time goes in v2:
time: 62.6 us; the launch traced here: 62.2 us
  Pallas kernels  53.3 us (85%)
  local copies, waits for them, and re-layouts  8.29 us (13%)
  between operations  0.66 us (1%)
    pallas_call x1, Pallas kernels, per_device(): pl.pallas_call(exchange_kernel, out_shape=(jax.ShapeDtypeStruct((32, 128)...  53.3 us
    unnamed x17, local copies, waits for them, and re-layouts  8.29 us

profile of v2, /device:TPU:1, one launch (start us, length us, event | category | flops | bytes accessed | tf_op | source)
XLA Modules:
  0.0 62.2 jit_solution(564499617786440525)
XLA Ops:
  0.6 0.0 copy-start
  0.6 1.6 %copy-done = bf16[32,64,512]{2,1,0:T(8,128)(2,1)S(1)} copy-done((bf16[32,64,512]{2,1,0:T(8,128)(2,1)S(1)}, bf16[32,64,512]{2,1,0:T(8,128)(2,1)}, u32[]{:S(2)}) %copy-start) | copy-done | bytes 2097176
  2.2 0.0 copy-start.1
  2.2 0.9 %copy-done.1 = bf16[512,256]{1,0:T(8,128)(2,1)S(1)} copy-done((bf16[512,256]{1,0:T(8,128)(2,1)S(1)}, bf16[512,256]{1,0:T(8,128)(2,1)}, u32[]{:S(2)}) %copy-start.1) | copy-done | bytes 262168
  3.2 0.0 copy-start.2
  3.2 0.9 %copy-done.2 = bf16[512,256]{1,0:T(8,128)(2,1)S(1)} copy-done((bf16[512,256]{1,0:T(8,128)(2,1)S(1)}, bf16[512,256]{1,0:T(8,128)(2,1)}, u32[]{:S(2)}) %copy-start.2) | copy-done | bytes 262168
  4.1 0.0 copy-start.3
  4.1 0.8 %copy-done.3 = bf16[64,256]{1,0:T(8,128)(2,1)S(1)} copy-done((bf16[64,256]{1,0:T(8,128)(2,1)S(1)}, bf16[64,256]{1,0:T(8,128)(2,1)}, u32[]{:S(2)}) %copy-start.3) | copy-done | bytes 32792
  4.9 0.0 copy-start.4
  4.9 0.7 %copy-done.4 = bf16[64,128]{1,0:T(8,128)(2,1)S(1)} copy-done((bf16[64,128]{1,0:T(8,128)(2,1)S(1)}, bf16[64,128]{1,0:T(8,128)(2,1)}, u32[]{:S(2)}) %copy-start.4) | copy-done | bytes 16408
  5.6 0.0 copy-start.5
  5.6 0.7 %copy-done.5 = bf16[32,128]{1,0:T(8,128)(2,1)S(1)} copy-done((bf16[32,128]{1,0:T(8,128)(2,1)S(1)}, bf16[32,128]{1,0:T(8,128)(2,1)}, u32[]{:S(2)}) %copy-start.5) | copy-done | bytes 8216
  6.3 0.0 copy-start.6
  6.3 0.7 %copy-done.6 = bf16[32,128]{1,0:T(8,128)(2,1)S(1)} copy-done((bf16[32,128]{1,0:T(8,128)(2,1)S(1)}, bf16[32,128]{1,0:T(8,128)(2,1)}, u32[]{:S(2)}) %copy-start.6) | copy-done | bytes 8216
  7.0 53.3 %exchange.1 = (f32[32,128]{1,0:T(8,128)S(1)}, f32[2,64,128]{2,1,0:T(8,128)S(1)}, f32[128,512]{1,0:T(8,128)S(1)}) custom-call(bf16[2048,512]{1,0:T(8,128)(2,1)S(1)} %bitcast.1, bf16[32,128]{1,0:T(8,128)(2,1)S(1)} %copy-done.5, bf16[32,128]{1,0:T(8,128)(2,1)S(1)} %copy-done.6, bf16[64,128]{1,0:T(8,128)(2,1)S(1)} %copy-done.4, bf16[64,256]{1,0:T(8,128)(2,1)S(1)} %copy-done.3, ...), custom_call_target="tpu_custom_call" | custom-call | tf_op jit(solution)/shard_map/exchange/pallas_call | solution.py:368
  60.3 0.6 copy.13
  60.9 0.6 %copy.14 = f32[2,64,128]{2,1,0:T(8,128)} copy(f32[2,64,128]{2,1,0:T(8,128)S(1)} %get-tuple-element.7) | data formatting | bytes 131072
  61.5 0.7 %copy.15 = f32[128,512]{1,0:T(8,128)} copy(f32[128,512]{1,0:T(8,128)S(1)} %get-tuple-element.8) | data formatting | bytes 524288
Async XLA Ops:
  0.6 1.6 %copy-start = (bf16[32,64,512]{2,1,0:T(8,128)(2,1)S(1)}, bf16[32,64,512]{2,1,0:T(8,128)(2,1)}, u32[]{:S(2)}) copy-start(bf16[32,64,512]{2,1,0:T(8,128)(2,1)} %param.7) | copy-start | bytes 6291460
  2.2 0.9 %copy-start.1 = (bf16[512,256]{1,0:T(8,128)(2,1)S(1)}, bf16[512,256]{1,0:T(8,128)(2,1)}, u32[]{:S(2)}) copy-start(bf16[512,256]{1,0:T(8,128)(2,1)} %right_m_hbm.1) | copy-start | bytes 786436
  3.2 0.9 %copy-start.2 = (bf16[512,256]{1,0:T(8,128)(2,1)S(1)}, bf16[512,256]{1,0:T(8,128)(2,1)}, u32[]{:S(2)}) copy-start(bf16[512,256]{1,0:T(8,128)(2,1)} %last_m_hbm.1) | copy-start | bytes 786436
  4.1 0.8 %copy-start.3 = (bf16[64,256]{1,0:T(8,128)(2,1)S(1)}, bf16[64,256]{1,0:T(8,128)(2,1)}, u32[]{:S(2)}) copy-start(bf16[64,256]{1,0:T(8,128)(2,1)} %right_y_hbm.1) | copy-start | bytes 98308
  4.9 0.7 %copy-start.4 = (bf16[64,128]{1,0:T(8,128)(2,1)S(1)}, bf16[64,128]{1,0:T(8,128)(2,1)}, u32[]{:S(2)}) copy-start(bf16[64,128]{1,0:T(8,128)(2,1)} %last_y_hbm.1) | copy-start | bytes 49156
  5.6 0.7 %copy-start.5 = (bf16[32,128]{1,0:T(8,128)(2,1)S(1)}, bf16[32,128]{1,0:T(8,128)(2,1)}, u32[]{:S(2)}) copy-start(bf16[32,128]{1,0:T(8,128)(2,1)} %left_x_hbm.1) | copy-start | bytes 24580
  6.3 0.7 %copy-start.6 = (bf16[32,128]{1,0:T(8,128)(2,1)S(1)}, bf16[32,128]{1,0:T(8,128)(2,1)}, u32[]{:S(2)}) copy-start(bf16[32,128]{1,0:T(8,128)(2,1)} %last_x_hbm.1) | copy-start | bytes 24580

commit v3 on v2

--- a/solution.py
+++ b/solution.py
@@ -379,7 +379,7 @@
         + [pltpu.VMEM(shape, f32) for shape in shapes]
         + [pltpu.SemaphoreType.DMA((count,)) for count in (COPIES, COPIES, 7)],
         compiler_params=pltpu.CompilerParams(
-            collective_id=0, has_side_effects=True, vmem_limit_bytes=32 * 1024 * 1024
+            collective_id=0, has_side_effects=True, vmem_limit_bytes=67_043_328
         ),
         name="exchange",
     )(*inputs)

time: 62.6 us -> 59.9 us (0.957)
  local copies, waits for them, and re-layouts: 8.29 us -> 4.47 us
  Pallas kernels: 53.3 us -> 54.5 us
    unnamed x17 -> x3, local copies, waits for them, and re-layouts: 8.29 us -> 4.47 us
    pallas_call x1, Pallas kernels: 53.3 us -> 54.5 us  [per_device(): pl.pallas_call(exchange_kernel, out_shape=(jax.ShapeDtypeStruct((32, 128)...]
where the time goes in v3:
time: 59.9 us; the launch traced here: 59.6 us
  Pallas kernels  54.5 us (91%)
  local copies, waits for them, and re-layouts  4.47 us (7%)
  between operations  0.64 us (1%)
    pallas_call x1, Pallas kernels, per_device(): pl.pallas_call(exchange_kernel, out_shape=(jax.ShapeDtypeStruct((32, 128)...  54.5 us
    unnamed x3, local copies, waits for them, and re-layouts  4.47 us

profile of v3, /device:TPU:1, one launch (start us, length us, event | category | flops | bytes accessed | tf_op | source)
XLA Modules:
  0.0 59.6 jit_solution(12952997138651702790)
XLA Ops:
  0.6 54.5 %exchange.1 = (f32[32,128]{1,0:T(8,128)}, f32[2,64,128]{2,1,0:T(8,128)}, f32[128,512]{1,0:T(8,128)}) custom-call(bf16[2048,512]{1,0:T(8,128)(2,1)} %bitcast.1, bf16[32,128]{1,0:T(8,128)(2,1)} %left_x_hbm.1, bf16[32,128]{1,0:T(8,128)(2,1)} %last_x_hbm.1, bf16[64,128]{1,0:T(8,128)(2,1)} %last_y_hbm.1, bf16[64,256]{1,0:T(8,128)(2,1)} %right_y_hbm.1, ...), custom_call_target="tpu_custom_call" | custom-call | tf_op jit(solution)/shard_map/exchange/pallas_call | solution.py:368
  55.2 1.3 %copy.13 = f32[32,128]{1,0:T(8,128)} copy(f32[32,128]{1,0:T(8,128)} %get-tuple-element.6) | data formatting | bytes 32768
  56.5 1.5 %copy.14 = f32[2,64,128]{2,1,0:T(8,128)} copy(f32[2,64,128]{2,1,0:T(8,128)} %get-tuple-element.7) | data formatting | bytes 131072
  58.0 1.7 %copy.15 = f32[128,512]{1,0:T(8,128)} copy(f32[128,512]{1,0:T(8,128)} %get-tuple-element.8) | data formatting | bytes 524288

commit v4 on v3

--- a/solution.py
+++ b/solution.py
@@ -50,19 +50,32 @@
     lane = lax.broadcasted_iota(jnp.int32, (size, size), 1)
     sub = lax.broadcasted_iota(jnp.int32, (size, size), 0)
 
-    def step(k, carry):
+    def step(n, carry):
+        k = 2 * n
         now = mat[...]
-        row = mat[pl.ds(k, 1), :]
-        here = lane == k
-        col = jnp.sum(jnp.where(here, now, 0.0), axis=1, keepdims=True)
-        pivot = jnp.sum(jnp.where(lane[:1] == k, row, 0.0), axis=1, keepdims=True)
-        inv = 1.0 / pivot
-        row_new = jnp.where(lane[:1] == k, 1.0, row) * inv
-        kept = jnp.where(here, 0.0, now)
-        mat[...] = jnp.where(sub == k, row_new, kept - col * row_new)
+        pair = mat[pl.ds(k, 2), :]
+        row0, row1 = pair[0:1], pair[1:2]
+        at0, at1 = lane == k, lane == k + 1
+        here0, here1 = at0[:1], at1[:1]
+        col0 = jnp.sum(jnp.where(at0, now, 0.0), axis=1, keepdims=True)
+        col1 = jnp.sum(jnp.where(at1, now, 0.0), axis=1, keepdims=True)
+        a = jnp.sum(jnp.where(here0, row0, 0.0), axis=1, keepdims=True)
+        b = jnp.sum(jnp.where(here1, row0, 0.0), axis=1, keepdims=True)
+        c = jnp.sum(jnp.where(here0, row1, 0.0), axis=1, keepdims=True)
+        d = jnp.sum(jnp.where(here1, row1, 0.0), axis=1, keepdims=True)
+        inv = 1.0 / a
+        ratio = c * inv
+        last_inv = 1.0 / (d - ratio * b)
+        unit0 = jnp.where(here0, 1.0, jnp.where(here1, 0.0, row0))
+        unit1 = jnp.where(here1, 1.0, jnp.where(here0, 0.0, row1))
+        new1 = (unit1 - ratio * unit0) * last_inv
+        new0 = (unit0 - b * new1) * inv
+        kept = jnp.where(at0 | at1, 0.0, now)
+        kept = kept - col0 * new0 - col1 * new1
+        mat[...] = jnp.where(sub == k, new0, jnp.where(sub == k + 1, new1, kept))
         return carry
 
-    lax.fori_loop(first, last, step, 0)
+    lax.fori_loop(first // 2, last // 2, step, 0)
 
 
 def exchange_kernel(
@@ -215,6 +228,7 @@
     y0s[...] = yf_ref[...] + y0[...]
     for d in (3, 0):
         t_sum(1, d)
+        t_zl[d] = send(ts.at[4 + d], t1.at[d], other_zl)
     for d in (1, 2, 3, 0):
         t_sum(0, d)
 
@@ -228,8 +242,6 @@
     for d in range(1, 8):
         z_z.append(send(z1s, z2.at[d], peer_z(d)[1]))
     y_zl = send(y0s, y1, other_zl)
-    for d in (3, 0):
-        t_zl[d] = send(ts.at[4 + d], t1.at[d], other_zl)
 
     for copy in c_xy:
         copy.wait_recv()

time: 59.9 us -> 64.1 us (1.070)
  Pallas kernels: 54.5 us -> 58.8 us
    pallas_call x1, Pallas kernels: 54.5 us -> 58.8 us  [per_device(): pl.pallas_call(exchange_kernel, out_shape=(jax.ShapeDtypeStruct((32, 128)...]
where the time goes in v4:
time: 64.1 us; the launch traced here: 63.9 us
  Pallas kernels  58.8 us (92%)
  local copies, waits for them, and re-layouts  4.47 us (7%)
    pallas_call x1, Pallas kernels, per_device(): pl.pallas_call(exchange_kernel, out_shape=(jax.ShapeDtypeStruct((32, 128)...  58.8 us
    unnamed x3, local copies, waits for them, and re-layouts  4.47 us

profile of v4, /device:TPU:1, one launch (start us, length us, event | category | flops | bytes accessed | tf_op | source)
XLA Modules:
  0.0 63.9 jit_solution(1269417919918148414)
XLA Ops:
  0.6 58.8 %exchange.1 = (f32[32,128]{1,0:T(8,128)}, f32[2,64,128]{2,1,0:T(8,128)}, f32[128,512]{1,0:T(8,128)}) custom-call(bf16[2048,512]{1,0:T(8,128)(2,1)} %bitcast.1, bf16[32,128]{1,0:T(8,128)(2,1)} %left_x_hbm.1, bf16[32,128]{1,0:T(8,128)(2,1)} %last_x_hbm.1, bf16[64,128]{1,0:T(8,128)(2,1)} %last_y_hbm.1, bf16[64,256]{1,0:T(8,128)(2,1)} %right_y_hbm.1, ...), custom_call_target="tpu_custom_call" | custom-call | tf_op jit(solution)/shard_map/exchange/pallas_call | solution.py:380
  59.4 1.3 %copy.13 = f32[32,128]{1,0:T(8,128)} copy(f32[32,128]{1,0:T(8,128)} %get-tuple-element.6) | data formatting | bytes 32768
  60.7 1.5 %copy.14 = f32[2,64,128]{2,1,0:T(8,128)} copy(f32[2,64,128]{2,1,0:T(8,128)} %get-tuple-element.7) | data formatting | bytes 131072
  62.2 1.7 %copy.15 = f32[128,512]{1,0:T(8,128)} copy(f32[128,512]{1,0:T(8,128)} %get-tuple-element.8) | data formatting | bytes 524288
